TPU v7x, 768 devices: a whole 4x8x12 slice. The times are simulated.
768 devices in a mesh: seq: 192 (over y, z, core), section: 4 (over x).
Axes of the slice: x: 4, y: 8, z: 12, core: 2. Of those that a mesh axis runs over, the one named last changes fastest.
Arguments:
- stream_in: bfloat16 [4, 24576, 2048], P('section', 'seq'), may hold values from -20 to 20
- keys_values: bfloat16 [4, 2, 24576, 512], P('section', None, 'seq'), may hold values from -6 to 6
- out_weight: bfloat16 [4, 2048, 2048], P('section'), may hold values from -1 to 1
- tile_mask: int32 [4, 16, 16], P('section'), may hold values 0 or 1
- cotangent: bfloat16 [4, 24576, 2048], P('section', 'seq'), may hold values from -6 to 6
Outputs:
- stream_out: bfloat16 [4, 24576, 2048], P('section', 'seq')
- stream_grads: bfloat16 [4, 24576, 2048], P('section', 'seq')
- kv_grads: float32 [4, 2, 24576, 512], P('section', None, 'seq')
All inputs are finite; a program needn't handle non-finite values. No bound on the sum of `tile_mask` on one device may be relied on, other than what follows from the above.
Results may differ from a plain program's by a relative error of at most 0.013.
Values may be sent and summed in bfloat16 or wider, within the bound.
A program may use at most 64 MiB of HBM per device.

v0:
```python
import jax
import jax.numpy as jnp
from jax import lax
from jax.sharding import PartitionSpec as P

HD = 128
TILE = 128
SPAN = 2


def from_behind(block, axis, distance):
    devices = range(lax.axis_size(axis))
    route = [(i - distance, i) for i in devices if i - distance in devices]
    return lax.ppermute(block, axis, route)


def from_behind_2(value, axis, by):
    length = lax.axis_size(axis)
    return lax.ppermute(value, axis, [(i, (i + by) % length) for i in range(length)])


def band_softmax(q_heads, key_rows, inside, scaling):
    logits = (
        jnp.einsum("rkgd,jkd->kgrj", q_heads, key_rows, preferred_element_type=jnp.float32)
        * scaling
    )
    logits = jnp.where(inside[None, None], logits, -jnp.inf)
    row_top = jnp.max(logits, axis=-1, keepdims=True)
    exp_terms = jnp.exp(logits - row_top)
    return exp_terms / jnp.sum(exp_terms, axis=-1, keepdims=True)


def per_device(stream_in, keys_values, out_weight, tile_mask, cotangent):
    queries = stream_in[0]
    tok_rows, row_width = queries.shape
    kv_width = keys_values.shape[-1]
    kv_heads = kv_width // HD
    group_size = row_width // HD // kv_heads
    span_shards = SPAN
    window = span_shards * tok_rows
    scaling = HD ** (-0.5)
    seq_index = lax.axis_index("seq")
    own_block = keys_values[0]
    pieces = [from_behind(own_block, "seq", offset + 1) for offset in range(span_shards)]
    kv_all = jnp.concatenate(pieces[::-1] + [own_block], axis=1)
    key_total = kv_all.shape[1]
    key_rows = kv_all[0].reshape(key_total, kv_heads, HD)
    value_rows = kv_all[1].reshape(key_total, kv_heads, HD)
    key_pos = (seq_index - span_shards) * tok_rows + jnp.arange(key_total, dtype=jnp.int32)
    tile_count = tile_mask.shape[1]
    shaped = out_weight[0].reshape(tile_count, TILE, tile_count, TILE)
    weight = jnp.where(tile_mask[0][:, None, :, None] > 0, shaped, jnp.zeros_like(shaped)).reshape(
        row_width, row_width
    )
    row_pos = seq_index * tok_rows + jnp.arange(tok_rows, dtype=jnp.int32)
    distance = row_pos[:, None] - key_pos[None, :]
    inside = (distance >= 0) & (distance < window) & (key_pos[None, :] >= 0)
    q_heads = queries.reshape(tok_rows, kv_heads, group_size, HD)
    probs = band_softmax(q_heads, key_rows, inside, scaling)
    prob_b = probs.astype(jnp.bfloat16)
    attended = jnp.einsum("kgrj,jkd->rkgd", prob_b, value_rows, preferred_element_type=jnp.float32)
    attended = attended.astype(jnp.bfloat16).reshape(tok_rows, row_width)
    mixed_rows = jnp.dot(attended, weight, preferred_element_type=jnp.float32)
    result = (queries.astype(jnp.float32) + mixed_rows).astype(jnp.bfloat16)
    next_input = from_behind_2(result, "section", 1)
    grad_in = cotangent[0]
    d_attended = lax.dot_general(
        grad_in, weight, (((1,), (1,)), ((), ())), preferred_element_type=jnp.float32
    )
    d_heads = d_attended.astype(jnp.bfloat16).reshape(tok_rows, kv_heads, group_size, HD)
    d_probs = jnp.einsum("rkgd,jkd->kgrj", d_heads, value_rows, preferred_element_type=jnp.float32)
    d_values = jnp.einsum("kgrj,rkgd->jkd", prob_b, d_heads, preferred_element_type=jnp.float32)
    row_dot = jnp.sum(probs * d_probs, axis=-1, keepdims=True)
    d_logits = (probs * (d_probs - row_dot)).astype(jnp.bfloat16)
    d_queries = (
        jnp.einsum("kgrj,jkd->rkgd", d_logits, key_rows, preferred_element_type=jnp.float32)
        * scaling
    )
    d_keys = (
        jnp.einsum("kgrj,rkgd->jkd", d_logits, q_heads, preferred_element_type=jnp.float32)
        * scaling
    )
    grad_out = (grad_in.astype(jnp.float32) + d_queries.reshape(tok_rows, row_width)).astype(
        jnp.bfloat16
    )
    prev_grad = from_behind_2(grad_out, "section", -1)
    kv_sum = jnp.stack([d_keys, d_values]).reshape(2, key_total, kv_width)
    shard_parts = [
        kv_sum[:, offset * tok_rows : (offset + 1) * tok_rows] for offset in range(span_shards + 1)
    ]
    kv_total = shard_parts[span_shards]
    for offset in range(1, span_shards + 1):
        kv_total = kv_total + from_behind(
            shard_parts[span_shards - offset].astype(jnp.bfloat16), "seq", -offset
        ).astype(jnp.float32)
    return (next_input[None], prev_grad[None], kv_total[None])


def solution(mesh):
    return jax.shard_map(
        per_device,
        mesh=mesh,
        in_specs=(
            P("section", "seq", None),
            P("section", None, "seq", None),
            P("section", None, None),
            P("section", None, None),
            P("section", "seq", None),
        ),
        out_specs=(
            P("section", "seq", None),
            P("section", "seq", None),
            P("section", None, "seq", None),
        ),
        check_vma=False,
    )
```

profile of v0, /device:TPU:54, one launch (start us, length us, event | category | flops | bytes accessed | tf_op | source)
XLA Modules:
  0.0 83.9 jit_solution(11226820094168721734)
XLA Ops:
  0.6 1.1 %copy.21 = bf16[1,2,128,512]{2,3,1,0:T(8,128)(2,1)S(1)} copy(bf16[1,2,128,512]{3,2,1,0:T(8,128)(2,1)} %param.6) | data formatting | bytes 524288 | tf_op args[1]
  1.8 4.3 %collective-permute-start = (bf16[2,128,512]{1,2,0:T(8,128)(2,1)S(1)}, bf16[2,128,512]{1,2,0:T(8,128)(2,1)S(1)}, u32[]{:S(2)}, u32[]{:S(2)}) collective-permute-start(bf16[2,128,512]{1,2,0:T(8,128)(2,1)S(1)} %bitcast.116), channel_id=1, source_target_pairs={{0,8},{4,12},{8,16},{12,20},{16,24},{20,28},{24,32},{28,36},{32,40... | collective-permute-start | bytes 786440 | tf_op jit(solution)/shard_map/ppermute | solution.py:14
  6.0 1.9 %collective-permute-start.1 = (bf16[2,128,512]{1,2,0:T(8,128)(2,1)S(1)}, bf16[2,128,512]{1,2,0:T(8,128)(2,1)S(1)}, u32[]{:S(2)}, u32[]{:S(2)}) collective-permute-start(bf16[2,128,512]{1,2,0:T(8,128)(2,1)S(1)} %bitcast.117), channel_id=1, source_target_pairs={{0,4},{4,8},{8,12},{12,16},{16,20},{20,24},{24,28},{28,32},{32,36}... | collective-permute-start | bytes 786440 | tf_op jit(solution)/shard_map/ppermute | solution.py:14
  8.0 0.0 copy-start.8
  8.0 9.8 %copy.50 = bf16[256,8,16,128]{3,2,1,0:T(8,128)(2,1)} copy(bf16[256,8,16,128]{3,1,2,0:T(8,128)(2,1)} %bitcast.107) | data formatting | bytes 16777216
  17.8 0.0 copy-done.8
  17.8 0.0 copy-start.6
  17.8 7.3 %bitcast_select_fusion = bf16[16,128,16,128]{3,2,1,0:T(8,128)(2,1)} fusion(pred[16,16]{1,0:T(8,128)(4,1)S(1)} %compare_bitcast_fusion, bf16[16,128,16,128]{3,2,1,0:T(8,128)(2,1)} %bitcast.106), kind=kLoop, calls=%fused_computation.5 | loop fusion | flops 4194304 | bytes 16777472 | tf_op jit(solution)/shard_map/jit(_where)/select_n | solution.py:52
  25.1 0.0 copy-done.6
  25.1 0.0 copy-start.4
  25.1 6.6 %fusion.13 = bf16[2048,128]{1,0:T(8,128)(2,1)} fusion(bf16[256,8,16,128]{3,2,1,0:T(8,128)(2,1)} %bitcast.108, bf16[1,128,2048]{2,1,0:T(8,128)(2,1)S(1)} %copy-done.6), kind=kOutput, calls=%fused_computation.16 | convolution fusion | flops 1074003968 | bytes 9437184 | tf_op jit(solution)/shard_map/dot_general | solution.py:67
  31.7 0.0 copy-done.4
  31.7 1.0 %copy.49 = bf16[1,128,2048]{1,2,0:T(8,128)(2,1)} copy(bf16[1,128,2048]{2,1,0:T(8,128)(2,1)S(1)} %copy-done.4) | data formatting | bytes 1048576 | tf_op jit(solution)/shard_map/reshape;squeeze | solution.py:58
  32.7 0.8 fusion.36
  33.5 0.0 collective-permute-done
  33.5 0.0 collective-permute-done.1
  33.5 0.1 pad_maximum_fusion.1
  33.6 0.8 fusion.40
  34.4 2.2 %fusion.41 = (f32[4,4,128]{2,1,0:T(4,128)S(1)}, f32[4,4,128,384]{2,3,1,0:T(8,128)S(1)}) fusion(pred[128,384]{0,1:T(8,128)(4,1)} %fusion.36, bf16[384,4,128,1]{0,2,3,1:T(8,128)(2,1)S(1)} %bitcast.114, bf16[128,4,4,128]{0,3,2,1:T(8,128)(2,1)} %bitcast.112), kind=kOutput, calls=%fused_computation.54 | convolution fusion | flops 204472704 | bytes 4120576 | tf_op jit(solution)/shard_map/sub | solution.py:29
  36.6 0.0 copy-start
  36.6 0.0 copy-start.7
  36.6 0.0 copy-start.9
  36.7 3.0 %fusion.25 = f32[4,128,384,1]{2,1,3,0:T(8,128)} fusion(bf16[128,4,4,128]{0,3,2,1:T(8,128)(2,1)} %bitcast.124, f32[4,4,128,384]{2,3,1,0:T(8,128)S(1)} %get-tuple-element.8, f32[4,4,128]{2,1,0:T(4,128)S(1)} %get-tuple-element.7), kind=kOutput, calls=%fused_computation.33 | convolution fusion | flops 202899456 | bytes 4464640 | tf_op jit(solution)/shard_map/kgrj,rkgd->jkd/dot_general | solution.py:72
  39.7 0.0 copy-done.7
  39.7 0.0 copy-done.9
  39.7 0.6 fusion.7
  40.3 0.0 copy-done
  40.3 0.0 copy-start.2
  40.3 0.5 fusion.9
  40.9 0.5 copy-done.2
  41.4 0.0 copy-start.1
  41.4 0.6 fusion.24
  42.0 0.4 convolution_multiply_fusion
  42.4 0.8 copy-done.1
  43.2 0.0 copy-start.3
  43.2 1.3 %convolution_convert_fusion = bf16[4,128,4,128]{3,1,2,0:T(8,128)(2,1)} fusion(bf16[384,4,128,1]{0,2,3,1:T(8,128)(2,1)S(1)} %bitcast.123, f32[4,4,128,384]{2,3,1,0:T(8,128)S(1)} %copy-done.1, f32[4,4,128]{2,1,0:T(4,128)S(1)} %get-tuple-element.7), kind=kOutput, calls=%fused_computation.29 | convolution fusion | flops 203161600 | bytes 4071424 | tf_op jit(solution)/shard_map/kgrj,jkd->rkgd/dot_general | solution.py:61
  44.5 0.3 copy.32
  44.8 0.0 copy-done.3
  44.8 0.3 copy.33
  45.1 0.0 copy-start.5
  45.1 1.4 %copy.28 = f32[128,2048]{1,0:T(8,128)} copy(f32[128,2048]{0,1:T(8,128)S(1)} %bitcast.110) | data formatting | bytes 2097152 | tf_op jit(solution)/shard_map/reshape | solution.py:83
  46.5 1.5 %add_convert_fusion = bf16[128,2048]{1,0:T(8,128)(2,1)S(1)} fusion(f32[128,2048]{1,0:T(8,128)} %copy.28, bf16[1,128,2048]{2,1,0:T(8,128)(2,1)} %param.9), kind=kLoop, calls=%fused_computation.31 | loop fusion | flops 786432 | bytes 2097152 | tf_op jit(solution)/shard_map/convert_element_type | solution.py:83
  48.0 2.7 %collective-permute-start.3 = (bf16[128,2048]{1,0:T(8,128)(2,1)S(1)}, bf16[128,2048]{1,0:T(8,128)(2,1)S(1)}, u32[]{:S(2)}, u32[]{:S(2)}) collective-permute-start(bf16[128,2048]{1,0:T(8,128)(2,1)S(1)} %add_convert_fusion), channel_id=1, source_target_pairs={{0,3},{1,0},{2,1},{3,2},{4,7},{5,4},{6,5},{7,6},{8,11},{9,8},{10,9... | collective-permute-start | bytes 1572872 | tf_op jit(solution)/shard_map/ppermute | solution.py:19
  50.7 0.0 copy-done.5
  50.7 4.9 %fusion.16 = bf16[128,2048]{1,0:T(8,128)(2,1)S(1)} fusion(bf16[128,2048]{0,1:T(8,128)(2,1)} %bitcast.126, bf16[256,8,16,128]{3,2,1,0:T(8,128)(2,1)} %bitcast.109, bf16[1,128,2048]{2,1,0:T(8,128)(2,1)S(1)} %copy-done.5), kind=kOutput, calls=%fused_computation.17 | convolution fusion | flops 1074528256 | bytes 9961472 | tf_op jit(solution)/shard_map/dot_general | solution.py:63
  55.6 4.3 %collective-permute-start.2 = (bf16[128,2048]{1,0:T(8,128)(2,1)S(1)}, bf16[128,2048]{1,0:T(8,128)(2,1)S(1)}, u32[]{:S(2)}, u32[]{:S(2)}) collective-permute-start(bf16[128,2048]{1,0:T(8,128)(2,1)S(1)} %fusion.16), channel_id=1, source_target_pairs={{0,1},{1,2},{2,3},{3,0},{4,5},{5,6},{6,7},{7,4},{8,9},{9,10},{10,1... | collective-permute-start | bytes 1572872 | tf_op jit(solution)/shard_map/ppermute | solution.py:19
  59.9 0.1 fusion.20
  60.1 11.9 %collective-permute-start.4 = (bf16[2,128,512]{2,1,0:T(8,128)(2,1)S(1)}, bf16[2,128,512]{2,1,0:T(8,128)(2,1)S(1)}, u32[]{:S(2)}, u32[]{:S(2)}) collective-permute-start(bf16[2,128,512]{2,1,0:T(8,128)(2,1)S(1)} %get-tuple-element.3), channel_id=1, source_target_pairs={{4,0},{8,4},{12,8},{16,12},{20,16},{24,20},{28,24},{32,28},{36,32}... | collective-permute-start | bytes 786440 | tf_op jit(solution)/shard_map/ppermute | solution.py:14
  72.0 4.2 %collective-permute-start.5 = (bf16[2,128,512]{2,1,0:T(8,128)(2,1)S(1)}, bf16[2,128,512]{2,1,0:T(8,128)(2,1)S(1)}, u32[]{:S(2)}, u32[]{:S(2)}) collective-permute-start(bf16[2,128,512]{2,1,0:T(8,128)(2,1)S(1)} %get-tuple-element.4), channel_id=1, source_target_pairs={{8,0},{12,4},{16,8},{20,12},{24,16},{28,20},{32,24},{36,28},{40,32... | collective-permute-start | bytes 786440 | tf_op jit(solution)/shard_map/ppermute | solution.py:14
  76.2 0.0 collective-permute-done.4
  76.2 5.3 %collective-permute-done.5 = bf16[2,128,512]{2,1,0:T(8,128)(2,1)S(1)} collective-permute-done((bf16[2,128,512]{2,1,0:T(8,128)(2,1)S(1)}, bf16[2,128,512]{2,1,0:T(8,128)(2,1)S(1)}, u32[]{:S(2)}, u32[]{:S(2)}) %collective-permute-start.5) | collective-permute-done | bytes 262176 | tf_op jit(solution)/shard_map/ppermute | solution.py:14
  81.5 0.9 %fusion.31 = f32[1,2,128,512]{3,2,1,0:T(8,128)} fusion(f32[1,384,512]{2,1,0:T(8,128)S(1)} %copy.32, f32[1,384,512]{2,1,0:T(8,128)S(1)} %copy.33, bf16[2,128,512]{2,1,0:T(8,128)(2,1)S(1)} %collective-permute-done.5, bf16[2,128,512]{2,1,0:T(8,128)(2,1)S(1)} %collective-permute-done.4), kind=kLoop, calls=%fused_computation.39 | loop fusion | flops 655360 | bytes 2621440 | tf_op jit(solution)/shard_map/broadcast_in_dim | solution.py:96
  82.4 0.0 collective-permute-done.3
  82.4 0.0 collective-permute-done.2
  82.4 0.8 copy.68
  83.2 0.8 copy.69
  (5 shorter events, 0.1 us)
Async XLA Ops:
  1.8 31.7 %collective-permute-start = (bf16[2,128,512]{1,2,0:T(8,128)(2,1)S(1)}, bf16[2,128,512]{1,2,0:T(8,128)(2,1)S(1)}, u32[]{:S(2)}, u32[]{:S(2)}) collective-permute-start(bf16[2,128,512]{1,2,0:T(8,128)(2,1)S(1)} %bitcast.116), channel_id=1, source_target_pairs={{0,8},{4,12},{8,16},{12,20},{16,24},{20,28},{24,32},{28,36},{32,40... | collective-permute-start | bytes 786440 | tf_op jit(solution)/shard_map/ppermute | solution.py:14
  6.0 27.4 %collective-permute-start.1 = (bf16[2,128,512]{1,2,0:T(8,128)(2,1)S(1)}, bf16[2,128,512]{1,2,0:T(8,128)(2,1)S(1)}, u32[]{:S(2)}, u32[]{:S(2)}) collective-permute-start(bf16[2,128,512]{1,2,0:T(8,128)(2,1)S(1)} %bitcast.117), channel_id=1, source_target_pairs={{0,4},{4,8},{8,12},{12,16},{16,20},{20,24},{24,28},{28,32},{32,36}... | collective-permute-start | bytes 786440 | tf_op jit(solution)/shard_map/ppermute | solution.py:14
  8.0 9.8 %copy-start.8 = (s32[1,16,16]{2,1,0:T(8,128)S(1)}, s32[1,16,16]{2,1,0:T(8,128)}, u32[]{:S(2)}) copy-start(s32[1,16,16]{2,1,0:T(8,128)} %param.8) | copy-start | bytes 3076
  17.8 7.3 %copy-start.6 = (bf16[1,128,2048]{2,1,0:T(8,128)(2,1)S(1)}, bf16[1,128,2048]{2,1,0:T(8,128)(2,1)}, u32[]{:S(2)}) copy-start(bf16[1,128,2048]{2,1,0:T(8,128)(2,1)} %param.9) | copy-start | bytes 1572868
  25.1 6.6 %copy-start.4 = (bf16[1,128,2048]{2,1,0:T(8,128)(2,1)S(1)}, bf16[1,128,2048]{2,1,0:T(8,128)(2,1)}, u32[]{:S(2)}) copy-start(bf16[1,128,2048]{2,1,0:T(8,128)(2,1)} %param.5) | copy-start | bytes 1572868
  36.6 3.7 %copy-start = (f32[4,4,128,384]{2,3,1,0:T(8,128)}, f32[4,4,128,384]{2,3,1,0:T(8,128)S(1)}, u32[]{:S(2)}) copy-start(f32[4,4,128,384]{2,3,1,0:T(8,128)S(1)} %get-tuple-element.8) | copy-start | bytes 9437188
  36.6 3.0 %copy-start.7 = (bf16[1,384,512]{1,2,0:T(8,128)(2,1)S(1)}, bf16[1,384,512]{1,2,0:T(8,128)(2,1)}, u32[]{:S(2)}) copy-start(bf16[1,384,512]{1,2,0:T(8,128)(2,1)} %get-tuple-element.6) | copy-start | bytes 1179652
  36.6 3.0 %copy-start.9 = (bf16[2048,128]{1,0:T(8,128)(2,1)S(1)}, bf16[2048,128]{1,0:T(8,128)(2,1)}, u32[]{:S(2)}) copy-start(bf16[2048,128]{1,0:T(8,128)(2,1)} %fusion.13) | copy-start | bytes 1572868
  40.3 1.0 %copy-start.2 = (bf16[1,128,2048]{1,2,0:T(8,128)(2,1)S(1)}, bf16[1,128,2048]{1,2,0:T(8,128)(2,1)}, u32[]{:S(2)}) copy-start(bf16[1,128,2048]{1,2,0:T(8,128)(2,1)} %copy.49) | copy-start | bytes 1572868
  41.4 1.9 %copy-start.1 = (f32[4,4,128,384]{2,3,1,0:T(8,128)S(1)}, f32[4,4,128,384]{2,3,1,0:T(8,128)}, u32[]{:S(2)}) copy-start(f32[4,4,128,384]{2,3,1,0:T(8,128)} %copy-done) | copy-start | bytes 9437188
  43.2 1.5 %copy-start.3 = (f32[4,128,384,1]{2,1,3,0:T(8,128)S(1)}, f32[4,128,384,1]{2,1,3,0:T(8,128)}, u32[]{:S(2)}) copy-start(f32[4,128,384,1]{2,1,3,0:T(8,128)} %fusion.25) | copy-start | bytes 2359300
  45.1 5.6 %copy-start.5 = (bf16[1,128,2048]{2,1,0:T(8,128)(2,1)S(1)}, bf16[1,128,2048]{2,1,0:T(8,128)(2,1)}, u32[]{:S(2)}) copy-start(bf16[1,128,2048]{2,1,0:T(8,128)(2,1)} %param.5) | copy-start | bytes 1572868
  48.0 34.4 %collective-permute-start.3 = (bf16[128,2048]{1,0:T(8,128)(2,1)S(1)}, bf16[128,2048]{1,0:T(8,128)(2,1)S(1)}, u32[]{:S(2)}, u32[]{:S(2)}) collective-permute-start(bf16[128,2048]{1,0:T(8,128)(2,1)S(1)} %add_convert_fusion), channel_id=1, source_target_pairs={{0,3},{1,0},{2,1},{3,2},{4,7},{5,4},{6,5},{7,6},{8,11},{9,8},{10,9... | collective-permute-start | bytes 1572872 | tf_op jit(solution)/shard_map/ppermute | solution.py:19
  55.6 26.8 %collective-permute-start.2 = (bf16[128,2048]{1,0:T(8,128)(2,1)S(1)}, bf16[128,2048]{1,0:T(8,128)(2,1)S(1)}, u32[]{:S(2)}, u32[]{:S(2)}) collective-permute-start(bf16[128,2048]{1,0:T(8,128)(2,1)S(1)} %fusion.16), channel_id=1, source_target_pairs={{0,1},{1,2},{2,3},{3,0},{4,5},{5,6},{6,7},{7,4},{8,9},{9,10},{10,1... | collective-permute-start | bytes 1572872 | tf_op jit(solution)/shard_map/ppermute | solution.py:19
  60.1 16.1 %collective-permute-start.4 = (bf16[2,128,512]{2,1,0:T(8,128)(2,1)S(1)}, bf16[2,128,512]{2,1,0:T(8,128)(2,1)S(1)}, u32[]{:S(2)}, u32[]{:S(2)}) collective-permute-start(bf16[2,128,512]{2,1,0:T(8,128)(2,1)S(1)} %get-tuple-element.3), channel_id=1, source_target_pairs={{4,0},{8,4},{12,8},{16,12},{20,16},{24,20},{28,24},{32,28},{36,32}... | collective-permute-start | bytes 786440 | tf_op jit(solution)/shard_map/ppermute | solution.py:14
  72.0 9.5 %collective-permute-start.5 = (bf16[2,128,512]{2,1,0:T(8,128)(2,1)S(1)}, bf16[2,128,512]{2,1,0:T(8,128)(2,1)S(1)}, u32[]{:S(2)}, u32[]{:S(2)}) collective-permute-start(bf16[2,128,512]{2,1,0:T(8,128)(2,1)S(1)} %get-tuple-element.4), channel_id=1, source_target_pairs={{8,0},{12,4},{16,8},{20,12},{24,16},{28,20},{32,24},{36,28},{40,32... | collective-permute-start | bytes 786440 | tf_op jit(solution)/shard_map/ppermute | solution.py:14
where the time goes:
time: 84.4 us; the launch traced here: 83.9 us
  starting transfers between devices  29.3 us (35%)
  matrix products  19.6 us (23%)
  local copies, waits for them, and re-layouts  17.6 us (21%)
  other arithmetic  11.2 us (13%)
  waiting for transfers between devices  5.28 us (6%)
  between operations  0.88 us (1%)
    ppermute x4, starting transfers between devices, from_behind(): return lax.ppermute(block, axis, route)  22.3 us
    unnamed x24, local copies, waits for them, and re-layouts  13.9 us
    select_n x1, other arithmetic, per_device(): jnp.where(tile_mask[0][:, None, :, None] > 0, shaped, jnp.zeros_like(shap...  7.27 us
    ppermute x2, starting transfers between devices, from_behind_2(): lax.ppermute(value, axis, [(i, (i + by) % length) for i in range(length)])  7.05 us
    dot_general x1, matrix products, per_device(): lax.dot_general(grad_in, weight, (((1,), (1,)), ((), ())), preferred_elem...  6.59 us
    ppermute x4, waiting for transfers between devices, from_behind(): return lax.ppermute(block, axis, route)  5.27 us
    dot_general x1, matrix products, per_device(): mixed_rows = jnp.dot(attended, weight, preferred_element_type=jnp.float32)  4.88 us
    dot_general x1, matrix products, per_device(): jnp.einsum('kgrj,rkgd->jkd', prob_b, d_heads, preferred_element_type=jnp....  3 us
  transfers between devices with their start and end apart: 6, of which 1 were waited for; matrix products, arithmetic and copies ran while one was open for 37% of the time, Pallas kernels for 0%

commit v1 on v0

v1 whole, which is shorter than its diff:
```python
import functools

import jax
import jax.numpy as jnp
from jax import lax
from jax.experimental import pallas as pl
from jax.experimental.pallas import tpu as pltpu
from jax.sharding import PartitionSpec as P

HD = 128
MESH = pl.DeviceIdType.MESH
NT = (((1,), (1,)), ((), ()))
NN = (((1,), (0,)), ((), ()))


def dot(a, b, dims=NN):
    return lax.dot_general(a, b, dims, preferred_element_type=jnp.float32)


def cols(start, count=1):
    return pl.ds(start * HD, count * HD)


def kernel(
    n_seq, n_sec,
    x_hbm, kv_hbm, w_hbm, mask, cot_hbm,
    so, sg, kvg,
    x, cot, w, kv, kvin, datt, att, gsend, osend, kvsend, kvrecv, kvacc,
    lsem, wsem, kv_s, kv_r, gkv_s, gkv_r, g_s, g_r, o_s, o_r,
):
    seq, sec = lax.axis_index("seq"), lax.axis_index("section")
    groups = kv.shape[2] // HD
    heads = x.shape[1] // HD // groups
    tiles = x.shape[1] // HD
    width = heads * HD
    scale = HD ** -0.5
    to_exp2 = scale * 1.4426950408889634
    ahead = [lax.rem(seq + 1, n_seq), lax.rem(seq + 2, n_seq)]
    behind = [lax.rem(seq + n_seq - 1, n_seq), lax.rem(seq + n_seq - 2, n_seq)]
    up, down = lax.rem(sec + 1, n_sec), lax.rem(sec + n_sec - 1, n_sec)

    loads = [
        pltpu.make_async_copy(kv_hbm.at[0], kv, lsem.at[0]),
        pltpu.make_async_copy(cot_hbm.at[0], cot, lsem.at[1]),
        pltpu.make_async_copy(x_hbm.at[0], x, lsem.at[2]),
    ]
    wloads = [
        pltpu.make_async_copy(w_hbm.at[0, cols(g * heads, heads)], w.at[cols(g * heads, heads)], wsem.at[g])
        for g in range(groups)
    ]
    for copy in loads + wloads:
        copy.start()

    barrier = pltpu.get_barrier_semaphore()
    for peer in ahead + behind:
        pl.semaphore_signal(barrier, inc=1, device_id={"seq": peer}, device_id_type=MESH)
    for peer in (up, down):
        pl.semaphore_signal(barrier, inc=1, device_id={"section": peer}, device_id_type=MESH)
    pl.semaphore_wait(barrier, 6)

    kv_out = [[None] * groups for _ in range(2)]
    for g in range(groups):
        for d in range(2):
            kv_out[d][g] = pltpu.make_async_remote_copy(
                src_ref=kv_hbm.at[0, :, :, cols(g)],
                dst_ref=kvin.at[d, :, :, cols(g)],
                send_sem=kv_s.at[d, g],
                recv_sem=kv_r.at[d, g],
                device_id={"seq": ahead[d]},
                device_id_type=MESH,
            )
            kv_out[d][g].start()

    loads[1].wait()
    cot_v = cot[...]
    for g in range(groups):
        wloads[g].wait()
        for a in range(g * heads, (g + 1) * heads):
            for b in range(tiles):
                keep = mask[0, a, b].astype(jnp.float32).astype(jnp.bfloat16)
                w[cols(a), cols(b)] = w[cols(a), cols(b)] * keep
        full = dot(w[cols(g * heads, heads), :], cot_v, NT).astype(jnp.bfloat16)
        for h in range(heads):
            datt[:, cols(g * heads + h)] = full[h * HD : (h + 1) * HD]

    loads[0].wait()
    loads[2].wait()
    key = lax.broadcasted_iota(jnp.int32, (HD, width), 0)
    tok = lax.broadcasted_iota(jnp.int32, (HD, width), 1) % HD
    own = key <= tok
    low = jnp.float32(-1e30)
    bias1 = jnp.where(seq >= 1, jnp.float32(0), low)
    bias2 = jnp.where(seq >= 2, jnp.float32(0), low)
    zero = jnp.zeros((HD, width), jnp.bfloat16)

    def split(block, prev):
        return jnp.concatenate(
            [jnp.where(own, block, zero), prev, jnp.where(own, zero, block)], axis=0
        )

    g_out, gkv_out = [], []

    def forward(g):
        for d in range(2):
            kv_out[d][g].wait_recv()
        ks = jnp.concatenate([kv[0, :, cols(g)], kvin[0, 0, :, cols(g)], kvin[1, 0, :, cols(g)]], axis=0)
        vs = jnp.concatenate([kv[1, :, cols(g)], kvin[0, 1, :, cols(g)], kvin[1, 1, :, cols(g)]], axis=0)
        qs = jnp.concatenate([x[:, cols(g * heads + h)] for h in range(heads)], axis=0)
        s = dot(ks, qs, NT)
        sc = jnp.where(own, s[:HD], s[2 * HD :] + bias2)
        s1 = s[HD : 2 * HD] + bias1
        top = jnp.maximum(jnp.max(sc, axis=0, keepdims=True), jnp.max(s1, axis=0, keepdims=True))
        ec = jnp.exp2((sc - top) * to_exp2)
        e1 = jnp.exp2((s1 - top) * to_exp2)
        inv = 1.0 / (jnp.sum(ec, axis=0, keepdims=True) + jnp.sum(e1, axis=0, keepdims=True))
        pc, p1 = ec * inv, e1 * inv
        pb = split(pc.astype(jnp.bfloat16), p1.astype(jnp.bfloat16))
        out_t = dot(vs.T, pb).astype(jnp.bfloat16)
        for h in range(heads):
            att[:, cols(g * heads + h)] = out_t[:, h * HD : (h + 1) * HD].T
        return ks, vs, qs, pc, p1, pb

    def backward(g, ks, vs, qs, pc, p1, pb):
        dt = datt[:, cols(g * heads, heads)]
        dp = dot(vs, dt)
        dc, d1 = jnp.where(own, dp[:HD], dp[2 * HD :]), dp[HD : 2 * HD]
        row = jnp.sum(pc * dc, axis=0, keepdims=True) + jnp.sum(p1 * d1, axis=0, keepdims=True)
        ds = split((pc * (dc - row)).astype(jnp.bfloat16), (p1 * (d1 - row)).astype(jnp.bfloat16))
        dq_t = dot(ks.T, ds) * scale
        for h in range(heads):
            at = cols(g * heads + h)
            gsend[:, at] = (cot[:, at].astype(jnp.float32) + dq_t[:, h * HD : (h + 1) * HD].T).astype(jnp.bfloat16)
        copy = pltpu.make_async_remote_copy(
            src_ref=gsend.at[:, cols(g * heads, heads)],
            dst_ref=sg.at[0, :, cols(g * heads, heads)],
            send_sem=g_s.at[g],
            recv_sem=g_r.at[g],
            device_id={"section": down},
            device_id_type=MESH,
        )
        copy.start()
        g_out.append(copy)
        both = [dot(ds, qs) * scale, dot(pb, dt, NT)]
        for i in range(2):
            kvacc[i, :, cols(g)] = both[i][:HD]
            for d in range(2):
                kvsend[d, i, :, cols(g)] = both[i][(d + 1) * HD : (d + 2) * HD].astype(jnp.bfloat16)
        for d in range(2):
            copy = pltpu.make_async_remote_copy(
                src_ref=kvsend.at[d, :, :, cols(g)],
                dst_ref=kvrecv.at[d, :, :, cols(g)],
                send_sem=gkv_s.at[d, g],
                recv_sem=gkv_r.at[d, g],
                device_id={"seq": behind[d]},
                device_id_type=MESH,
            )
            copy.start()
            gkv_out.append(copy)

    for g in range(groups - 1):
        backward(g, *forward(g))
    held = forward(groups - 1)
    o_out = []
    for c in range(groups):
        at = cols(c * heads, heads)
        osend[:, at] = (x[:, at].astype(jnp.float32) + dot(att[...], w[:, at])).astype(jnp.bfloat16)
        copy = pltpu.make_async_remote_copy(
            src_ref=osend.at[:, at],
            dst_ref=so.at[0, :, at],
            send_sem=o_s.at[c],
            recv_sem=o_r.at[c],
            device_id={"section": up},
            device_id_type=MESH,
        )
        copy.start()
        o_out.append(copy)
    backward(groups - 1, *held)

    for copy in gkv_out:
        copy.wait_recv()
    kvg[0] = kvacc[...] + kvrecv[0].astype(jnp.float32) + kvrecv[1].astype(jnp.float32)
    for copy in kv_out[0] + kv_out[1] + gkv_out:
        copy.wait_send()
    for copy in g_out + o_out:
        copy.wait()


def solution(mesh):
    n_seq, n_sec = mesh.shape["seq"], mesh.shape["section"]

    def per_device(x, kv, w, mask, cot):
        _, rows, hid = x.shape
        kvw = kv.shape[-1]
        groups = kvw // HD
        bf, f32 = jnp.bfloat16, jnp.float32
        dma = pltpu.SemaphoreType.DMA
        vmem = pl.BlockSpec(memory_space=pltpu.VMEM)
        hbm = pl.BlockSpec(memory_space=pl.ANY)
        return pl.pallas_call(
            functools.partial(kernel, n_seq, n_sec),
            out_shape=(
                jax.ShapeDtypeStruct((1, rows, hid), bf),
                jax.ShapeDtypeStruct((1, rows, hid), bf),
                jax.ShapeDtypeStruct((1, 2, rows, kvw), f32),
            ),
            in_specs=[hbm, hbm, hbm, pl.BlockSpec(memory_space=pltpu.SMEM), hbm],
            out_specs=(vmem, vmem, vmem),
            scratch_shapes=[
                pltpu.VMEM((rows, hid), bf),
                pltpu.VMEM((rows, hid), bf),
                pltpu.VMEM((hid, hid), bf),
                pltpu.VMEM((2, rows, kvw), bf),
                pltpu.VMEM((2, 2, rows, kvw), bf),
                pltpu.VMEM((rows, hid), bf),
                pltpu.VMEM((rows, hid), bf),
                pltpu.VMEM((rows, hid), bf),
                pltpu.VMEM((rows, hid), bf),
                pltpu.VMEM((2, 2, rows, kvw), bf),
                pltpu.VMEM((2, 2, rows, kvw), bf),
                pltpu.VMEM((2, rows, kvw), f32),
                dma((3,)),
                dma((groups,)),
                dma((2, groups)),
                dma((2, groups)),
                dma((2, groups)),
                dma((2, groups)),
                dma((groups,)),
                dma((groups,)),
                dma((groups,)),
                dma((groups,)),
            ],
            compiler_params=pltpu.CompilerParams(
                collective_id=0, has_side_effects=True, vmem_limit_bytes=60 * 1024 * 1024
            ),
        )(x, kv, w, mask, cot)

    return jax.shard_map(
        per_device,
        mesh=mesh,
        in_specs=(
            P("section", "seq", None),
            P("section", None, "seq", None),
            P("section", None, None),
            P("section", None, None),
            P("section", "seq", None),
        ),
        out_specs=(
            P("section", "seq", None),
            P("section", "seq", None),
            P("section", None, "seq", None),
        ),
        check_vma=False,
    )
```

time: 84.4 us -> 51.8 us (0.61)
  the two profiles are of different devices: /device:TPU:54 before, /device:TPU:1 now
where the time goes in v1:
time: 51.8 us; the launch traced here: 51.5 us
  Pallas kernels  45.2 us (87%)
  local copies, waits for them, and re-layouts  5.63 us (11%)
  between operations  0.64 us (1%)
    pallas_call x1, Pallas kernels, per_device(): pl.pallas_call(functools.partial(kernel, n_seq, n_sec), out_shape=(jax.Sh...  45.2 us
    unnamed x3, local copies, waits for them, and re-layouts  5.63 us

profile of v1, /device:TPU:1, one launch (start us, length us, event | category | flops | bytes accessed | tf_op | source)
XLA Modules:
  0.0 51.5 jit_solution(7404590411461678307)
XLA Ops:
  0.6 45.2 %shard_map.76 = (bf16[1,128,2048]{2,1,0:T(8,128)(2,1)}, bf16[1,128,2048]{2,1,0:T(8,128)(2,1)}, f32[1,2,128,512]{3,2,1,0:T(8,128)}) custom-call(bf16[1,128,2048]{2,1,0:T(8,128)(2,1)} %x_hbm.1, bf16[1,2,128,512]{3,2,1,0:T(8,128)(2,1)} %kv_hbm.1, bf16[1,2048,2048]{2,1,0:T(8,128)(2,1)} %w_hbm.1, s32[1,16,16]{2,1,0:T(8,128)} %mask.1, bf16[1,128,2048]{2,1,0:T(8,128)(2,1)} %cot_hbm.1), custom_call_target="tpu_custom_call" | custom-call | tf_op jit(solution)/shard_map/pallas_call | solution.py:199
  45.9 1.9 %copy.11 = bf16[1,128,2048]{2,1,0:T(8,128)(2,1)} copy(bf16[1,128,2048]{2,1,0:T(8,128)(2,1)} %get-tuple-element.6) | data formatting | bytes 1048576
  47.8 1.9 %copy.12 = bf16[1,128,2048]{2,1,0:T(8,128)(2,1)} copy(bf16[1,128,2048]{2,1,0:T(8,128)(2,1)} %get-tuple-element.7) | data formatting | bytes 1048576
  49.6 1.9 %copy.13 = f32[1,2,128,512]{3,2,1,0:T(8,128)} copy(f32[1,2,128,512]{3,2,1,0:T(8,128)} %get-tuple-element.8) | data formatting | bytes 1048576

commit v2 on v1

--- a/solution.py
+++ b/solution.py
@@ -11,6 +11,9 @@
 MESH = pl.DeviceIdType.MESH
 NT = (((1,), (1,)), ((), ()))
 NN = (((1,), (0,)), ((), ()))
+EVEN_AFTER = 1
+ARRIVE = 0
+ORDER = [(step, int(g)) for step, g in zip("ffffobobobob", "012300112233")]
 
 
 def dot(a, b, dims=NN):
@@ -35,8 +38,16 @@
     width = heads * HD
     scale = HD ** -0.5
     to_exp2 = scale * 1.4426950408889634
-    ahead = [lax.rem(seq + 1, n_seq), lax.rem(seq + 2, n_seq)]
-    behind = [lax.rem(seq + n_seq - 1, n_seq), lax.rem(seq + n_seq - 2, n_seq)]
+    even = lax.rem(seq, 2) == 0
+    odd = lax.rem(seq, 2) == 1
+    has_next = seq + 2 < n_seq
+    has_prev = seq >= 2
+    mate = seq + 1 - 2 * lax.rem(seq, 2)
+    ahead = lax.rem(seq + 2, n_seq)
+    behind = lax.rem(seq + n_seq - 2, n_seq)
+    before = lax.rem(seq + n_seq - 1, n_seq)
+    cross = lax.rem(seq + n_seq + 2 * lax.rem(seq, 2) - 1, n_seq)
+    has_cross = (even & has_prev) | (odd & has_next)
     up, down = lax.rem(sec + 1, n_sec), lax.rem(sec + n_sec - 1, n_sec)
 
     loads = [
@@ -52,24 +63,57 @@
         copy.start()
 
     barrier = pltpu.get_barrier_semaphore()
-    for peer in ahead + behind:
+
+    def greet(peer):
         pl.semaphore_signal(barrier, inc=1, device_id={"seq": peer}, device_id_type=MESH)
+
+    greet(mate)
+    for there, peer in ((has_next, ahead), (has_prev, behind), (has_cross, cross)):
+        pl.when(there)(functools.partial(greet, peer))
     for peer in (up, down):
         pl.semaphore_signal(barrier, inc=1, device_id={"section": peer}, device_id_type=MESH)
-    pl.semaphore_wait(barrier, 6)
-
-    kv_out = [[None] * groups for _ in range(2)]
-    for g in range(groups):
-        for d in range(2):
-            kv_out[d][g] = pltpu.make_async_remote_copy(
-                src_ref=kv_hbm.at[0, :, :, cols(g)],
-                dst_ref=kvin.at[d, :, :, cols(g)],
-                send_sem=kv_s.at[d, g],
-                recv_sem=kv_r.at[d, g],
-                device_id={"seq": ahead[d]},
-                device_id_type=MESH,
-            )
-            kv_out[d][g].start()
+    one = [there.astype(jnp.int32) for there in (has_next, has_prev, has_cross)]
+    pl.semaphore_wait(barrier, 3 + one[0] + one[1] + one[2])
+
+    def kv_copy(d, g, src, peer):
+        return pltpu.make_async_remote_copy(
+            src_ref=src,
+            dst_ref=kvin.at[d, :, :, cols(g)],
+            send_sem=kv_s.at[d, g],
+            recv_sem=kv_r.at[d, g],
+            device_id={"seq": peer},
+            device_id_type=MESH,
+        )
+
+    direct = [kv_copy(0, g, kv_hbm.at[0, :, :, cols(g)], mate) for g in range(groups)]
+    relay = [kv_copy(0, g, kvin.at[1, :, :, cols(g)], mate) for g in range(groups)]
+    hop = [kv_copy(1, g, kv_hbm.at[0, :, :, cols(g)], ahead) for g in range(groups)]
+
+    @pl.when(odd & has_next)
+    def _():
+        for copy in hop:
+            copy.start()
+
+    @pl.when(even)
+    def _():
+        for copy in direct:
+            copy.start()
+
+    @pl.when(jnp.logical_not(has_prev))
+    def _():
+        kvin[1] = jnp.zeros(kvin.shape[1:], kvin.dtype)
+
+    @pl.when(seq == 0)
+    def _():
+        kvin[0] = jnp.zeros(kvin.shape[1:], kvin.dtype)
+
+    @pl.when(jnp.logical_not(has_next))
+    def _():
+        kvrecv[1] = jnp.zeros(kvrecv.shape[1:], kvrecv.dtype)
+
+    @pl.when(odd & jnp.logical_not(has_next))
+    def _():
+        kvrecv[0] = jnp.zeros(kvrecv.shape[1:], kvrecv.dtype)
 
     loads[1].wait()
     cot_v = cot[...]
@@ -82,6 +126,11 @@
         full = dot(w[cols(g * heads, heads), :], cot_v, NT).astype(jnp.bfloat16)
         for h in range(heads):
             datt[:, cols(g * heads + h)] = full[h * HD : (h + 1) * HD]
+        if g == EVEN_AFTER:
+            @pl.when(even & has_next)
+            def _():
+                for copy in hop:
+                    copy.start()
 
     loads[0].wait()
     loads[2].wait()
@@ -100,9 +149,27 @@
 
     g_out, gkv_out = [], []
 
+    arrived = []
+
+    def arrive(upto):
+        for g in range(len(arrived), max(upto + 1, ARRIVE)):
+            arrived.append(g)
+
+            @pl.when(has_prev)
+            def _():
+                hop[g].wait_recv()
+
+            @pl.when(odd & has_prev)
+            def _():
+                relay[g].start()
+
     def forward(g):
-        for d in range(2):
-            kv_out[d][g].wait_recv()
+        arrive(g)
+
+        @pl.when(even & has_prev | odd)
+        def _():
+            direct[g].wait_recv()
+
         ks = jnp.concatenate([kv[0, :, cols(g)], kvin[0, 0, :, cols(g)], kvin[1, 0, :, cols(g)]], axis=0)
         vs = jnp.concatenate([kv[1, :, cols(g)], kvin[0, 1, :, cols(g)], kvin[1, 1, :, cols(g)]], axis=0)
         qs = jnp.concatenate([x[:, cols(g * heads + h)] for h in range(heads)], axis=0)
@@ -145,23 +212,22 @@
             kvacc[i, :, cols(g)] = both[i][:HD]
             for d in range(2):
                 kvsend[d, i, :, cols(g)] = both[i][(d + 1) * HD : (d + 2) * HD].astype(jnp.bfloat16)
-        for d in range(2):
-            copy = pltpu.make_async_remote_copy(
+        pair = [
+            pltpu.make_async_remote_copy(
                 src_ref=kvsend.at[d, :, :, cols(g)],
                 dst_ref=kvrecv.at[d, :, :, cols(g)],
                 send_sem=gkv_s.at[d, g],
                 recv_sem=gkv_r.at[d, g],
-                device_id={"seq": behind[d]},
+                device_id={"seq": (before, behind)[d]},
                 device_id_type=MESH,
             )
-            copy.start()
-            gkv_out.append(copy)
-
-    for g in range(groups - 1):
-        backward(g, *forward(g))
-    held = forward(groups - 1)
-    o_out = []
-    for c in range(groups):
+            for d in range(2)
+        ]
+        pl.when(odd | has_prev)(pair[0].start)
+        pl.when(has_prev)(pair[1].start)
+        gkv_out.append(pair)
+
+    def project(c):
         at = cols(c * heads, heads)
         osend[:, at] = (x[:, at].astype(jnp.float32) + dot(att[...], w[:, at])).astype(jnp.bfloat16)
         copy = pltpu.make_async_remote_copy(
@@ -174,14 +240,60 @@
         )
         copy.start()
         o_out.append(copy)
-    backward(groups - 1, *held)
-
-    for copy in gkv_out:
-        copy.wait_recv()
+
+    o_out, held = [], {}
+    for step, g in ORDER:
+        if step == "f":
+            held[g] = forward(g)
+        elif step == "b":
+            backward(g, *held.pop(g))
+        else:
+            project(g)
+
+    @pl.when(even | has_next)
+    def _():
+        for pair in gkv_out:
+            pair[0].wait_recv()
+
+    @pl.when(has_next)
+    def _():
+        for pair in gkv_out:
+            pair[1].wait_recv()
+
     kvg[0] = kvacc[...] + kvrecv[0].astype(jnp.float32) + kvrecv[1].astype(jnp.float32)
-    for copy in kv_out[0] + kv_out[1] + gkv_out:
-        copy.wait_send()
+
+    @pl.when(even | has_prev)
+    def _():
+        for copy in direct:
+            copy.wait_send()
+
+    @pl.when(has_next)
+    def _():
+        for copy in hop:
+            copy.wait_send()
+
+    @pl.when(odd | has_prev)
+    def _():
+        for pair in gkv_out:
+            pair[0].wait_send()
+
+    @pl.when(has_prev)
+    def _():
+        for pair in gkv_out:
+            pair[1].wait_send()
+
     for copy in g_out + o_out:
+        copy.wait()
+
+
+def store(a, b, c, a_out, b_out, c_out, sem):
+    copies = [
+        pltpu.make_async_copy(src, dst, sem.at[i])
+        for i, (src, dst) in enumerate([(a, a_out), (b, b_out), (c, c_out)])
+    ]
+    for copy in copies:
+        copy.start()
+    for copy in copies:
         copy.wait()
 
 
@@ -196,12 +308,12 @@
         dma = pltpu.SemaphoreType.DMA
         vmem = pl.BlockSpec(memory_space=pltpu.VMEM)
         hbm = pl.BlockSpec(memory_space=pl.ANY)
-        return pl.pallas_call(
+        outs = pl.pallas_call(
             functools.partial(kernel, n_seq, n_sec),
             out_shape=(
-                jax.ShapeDtypeStruct((1, rows, hid), bf),
-                jax.ShapeDtypeStruct((1, rows, hid), bf),
-                jax.ShapeDtypeStruct((1, 2, rows, kvw), f32),
+                pltpu.VMEM((1, rows, hid), bf),
+                pltpu.VMEM((1, rows, hid), bf),
+                pltpu.VMEM((1, 2, rows, kvw), f32),
             ),
             in_specs=[hbm, hbm, hbm, pl.BlockSpec(memory_space=pltpu.SMEM), hbm],
             out_specs=(vmem, vmem, vmem),
@@ -233,6 +345,13 @@
                 collective_id=0, has_side_effects=True, vmem_limit_bytes=60 * 1024 * 1024
             ),
         )(x, kv, w, mask, cot)
+        return pl.pallas_call(
+            store,
+            out_shape=tuple(jax.ShapeDtypeStruct(o.shape, o.dtype) for o in outs),
+            in_specs=[hbm] * 3,
+            out_specs=(hbm,) * 3,
+            scratch_shapes=[dma((3,))],
+        )(*(pltpu.with_memory_space_constraint(o, pltpu.VMEM) for o in outs))
 
     return jax.shard_map(
         per_device,

time: 51.8 us -> 39.9 us (0.77)
  the two profiles are of different devices: /device:TPU:1 before, /device:TPU:40 now
where the time goes in v2:
time: 39.9 us; the launch traced here: 39.7 us
  Pallas kernels  39.1 us (98%)
  between operations  0.64 us (2%)
    pallas_call x1, Pallas kernels, per_device(): pl.pallas_call(functools.partial(kernel, n_seq, n_sec), out_shape=(pltpu....  37.9 us
    pallas_call x1, Pallas kernels, per_device(): pl.pallas_call(store, out_shape=tuple((jax.ShapeDtypeStruct(o.shape, o.dt...  1.17 us

profile of v2, /device:TPU:40, one launch (start us, length us, event | category | flops | bytes accessed | tf_op | source)
XLA Modules:
  0.0 39.7 jit_solution(1109828385885143726)
XLA Ops:
  0.6 37.9 %shard_map.76 = (bf16[1,128,2048]{2,1,0:T(8,128)(2,1)S(1)}, bf16[1,128,2048]{2,1,0:T(8,128)(2,1)S(1)}, f32[1,2,128,512]{3,2,1,0:T(8,128)S(1)}) custom-call(bf16[1,128,2048]{2,1,0:T(8,128)(2,1)} %x_hbm.1, bf16[1,2,128,512]{3,2,1,0:T(8,128)(2,1)} %kv_hbm.1, bf16[1,2048,2048]{2,1,0:T(8,128)(2,1)} %w_hbm.1, s32[1,16,16]{2,1,0:T(8,128)} %mask.1, ...), custom_call_target="tpu_custom_call" | custom-call | tf_op jit(solution)/shard_map/pallas_call | solution.py:311
  38.6 1.2 %shard_map.77 = (bf16[1,128,2048]{2,1,0:T(8,128)(2,1)}, bf16[1,128,2048]{2,1,0:T(8,128)(2,1)}, f32[1,2,128,512]{3,2,1,0:T(8,128)}) custom-call(bf16[1,128,2048]{2,1,0:T(8,128)(2,1)S(1)} %get-tuple-element.6.a, bf16[1,128,2048]{2,1,0:T(8,128)(2,1)S(1)} %get-tuple-element.7.b, f32[1,2,128,512]{3,2,1,0:T(8,128)S(1)} %get-tuple-element.8.c), custom_call_target="tpu_custom_call" | custom-call | tf_op jit(solution)/shard_map/pallas_call | solution.py:348

commit v3 on v2

--- a/solution.py
+++ b/solution.py
@@ -11,9 +11,16 @@
 MESH = pl.DeviceIdType.MESH
 NT = (((1,), (1,)), ((), ()))
 NN = (((1,), (0,)), ((), ()))
-EVEN_AFTER = 1
-ARRIVE = 0
-ORDER = [(step, int(g)) for step, g in zip("ffffobobobob", "012300112233")]
+SLAB = 4
+
+
+def steps(names, groups):
+    return [(name, int(group)) for name, group in zip(names, groups)]
+
+
+FIRST = steps("dde", "010")
+EVEN = steps("ddfbfbfbfboooo", "23001122330123")
+ODD = steps("ffffobobdobdob", "01230011222333")
 
 
 def dot(a, b, dims=NN):
@@ -26,9 +33,9 @@
 
 def kernel(
     n_seq, n_sec,
-    x_hbm, kv_hbm, w_hbm, mask, cot_hbm,
+    x_hbm, kv_hbm, w_hbm, mask_hbm, cot_hbm,
     so, sg, kvg,
-    x, cot, w, kv, kvin, datt, att, gsend, osend, kvsend, kvrecv, kvacc,
+    mask, x, cot, w, kv, kvin, datt, att, gsend, osend, kvsend, kvrecv, kvacc,
     lsem, wsem, kv_s, kv_r, gkv_s, gkv_r, g_s, g_r, o_s, o_r,
 ):
     seq, sec = lax.axis_index("seq"), lax.axis_index("section")
@@ -54,10 +61,11 @@
         pltpu.make_async_copy(kv_hbm.at[0], kv, lsem.at[0]),
         pltpu.make_async_copy(cot_hbm.at[0], cot, lsem.at[1]),
         pltpu.make_async_copy(x_hbm.at[0], x, lsem.at[2]),
+        pltpu.make_async_copy(mask_hbm, mask, lsem.at[3]),
     ]
     wloads = [
-        pltpu.make_async_copy(w_hbm.at[0, cols(g * heads, heads)], w.at[cols(g * heads, heads)], wsem.at[g])
-        for g in range(groups)
+        pltpu.make_async_copy(w_hbm.at[0, cols(i * SLAB, SLAB)], w.at[cols(i * SLAB, SLAB)], wsem.at[i])
+        for i in range(tiles // SLAB)
     ]
     for copy in loads + wloads:
         copy.start()
@@ -115,25 +123,34 @@
     def _():
         kvrecv[0] = jnp.zeros(kvrecv.shape[1:], kvrecv.dtype)
 
+    loads[3].wait()
     loads[1].wait()
-    cot_v = cot[...]
-    for g in range(groups):
-        wloads[g].wait()
+    pruned, landed = set(), set()
+
+    def prune(a, c):
+        if a // SLAB not in landed:
+            landed.add(a // SLAB)
+            wloads[a // SLAB].wait()
+        if (a, c) in pruned:
+            return
+        pruned.add((a, c))
+        for b in range(c * heads, (c + 1) * heads):
+            keep = mask[0, a, b].astype(jnp.float32).astype(jnp.bfloat16)
+            w[cols(a), cols(b)] = w[cols(a), cols(b)] * keep
+
+    def attended_grad(g):
         for a in range(g * heads, (g + 1) * heads):
-            for b in range(tiles):
-                keep = mask[0, a, b].astype(jnp.float32).astype(jnp.bfloat16)
-                w[cols(a), cols(b)] = w[cols(a), cols(b)] * keep
-        full = dot(w[cols(g * heads, heads), :], cot_v, NT).astype(jnp.bfloat16)
-        for h in range(heads):
-            datt[:, cols(g * heads + h)] = full[h * HD : (h + 1) * HD]
-        if g == EVEN_AFTER:
-            @pl.when(even & has_next)
-            def _():
-                for copy in hop:
-                    copy.start()
-
-    loads[0].wait()
-    loads[2].wait()
+            for c in range(groups):
+                prune(a, c)
+        at = cols(g * heads, heads)
+        datt[:, at] = dot(cot[...], w[at, :], NT).astype(jnp.bfloat16)
+
+    def send_even():
+        @pl.when(even & has_next)
+        def _():
+            for copy in hop:
+                copy.start()
+
     key = lax.broadcasted_iota(jnp.int32, (HD, width), 0)
     tok = lax.broadcasted_iota(jnp.int32, (HD, width), 1) % HD
     own = key <= tok
@@ -147,29 +164,45 @@
             [jnp.where(own, block, zero), prev, jnp.where(own, zero, block)], axis=0
         )
 
-    g_out, gkv_out = [], []
-
-    arrived = []
-
-    def arrive(upto):
-        for g in range(len(arrived), max(upto + 1, ARRIVE)):
-            arrived.append(g)
-
-            @pl.when(has_prev)
-            def _():
-                hop[g].wait_recv()
-
-            @pl.when(odd & has_prev)
-            def _():
+    def strip(src, dst, sems, g, peer):
+        at = cols(g * heads, heads)
+        return pltpu.make_async_remote_copy(
+            src_ref=src.at[:, at],
+            dst_ref=dst.at[0, :, at],
+            send_sem=sems[0].at[g],
+            recv_sem=sems[1].at[g],
+            device_id={"section": peer},
+            device_id_type=MESH,
+        )
+
+    g_out = [strip(gsend, sg, (g_s, g_r), g, down) for g in range(groups)]
+    o_out = [strip(osend, so, (o_s, o_r), g, up) for g in range(groups)]
+    gkv_out = [
+        [
+            pltpu.make_async_remote_copy(
+                src_ref=kvsend.at[d, :, :, cols(g)],
+                dst_ref=kvrecv.at[d, :, :, cols(g)],
+                send_sem=gkv_s.at[d, g],
+                recv_sem=gkv_r.at[d, g],
+                device_id={"seq": (before, behind)[d]},
+                device_id_type=MESH,
+            )
+            for d in range(2)
+        ]
+        for g in range(groups)
+    ]
+
+    def forward(parity, g):
+        @pl.when(has_prev)
+        def _():
+            hop[g].wait_recv()
+            if parity:
                 relay[g].start()
-
-    def forward(g):
-        arrive(g)
-
-        @pl.when(even & has_prev | odd)
-        def _():
+            else:
+                direct[g].wait_recv()
+
+        if parity:
             direct[g].wait_recv()
-
         ks = jnp.concatenate([kv[0, :, cols(g)], kvin[0, 0, :, cols(g)], kvin[1, 0, :, cols(g)]], axis=0)
         vs = jnp.concatenate([kv[1, :, cols(g)], kvin[0, 1, :, cols(g)], kvin[1, 1, :, cols(g)]], axis=0)
         qs = jnp.concatenate([x[:, cols(g * heads + h)] for h in range(heads)], axis=0)
@@ -187,9 +220,9 @@
             att[:, cols(g * heads + h)] = out_t[:, h * HD : (h + 1) * HD].T
         return ks, vs, qs, pc, p1, pb
 
-    def backward(g, ks, vs, qs, pc, p1, pb):
-        dt = datt[:, cols(g * heads, heads)]
-        dp = dot(vs, dt)
+    def backward(parity, g, ks, vs, qs, pc, p1, pb):
+        dt = jnp.concatenate([datt[:, cols(g * heads + h)] for h in range(heads)], axis=0)
+        dp = dot(vs, dt, NT)
         dc, d1 = jnp.where(own, dp[:HD], dp[2 * HD :]), dp[HD : 2 * HD]
         row = jnp.sum(pc * dc, axis=0, keepdims=True) + jnp.sum(p1 * d1, axis=0, keepdims=True)
         ds = split((pc * (dc - row)).astype(jnp.bfloat16), (p1 * (d1 - row)).astype(jnp.bfloat16))
@@ -197,70 +230,66 @@
         for h in range(heads):
             at = cols(g * heads + h)
             gsend[:, at] = (cot[:, at].astype(jnp.float32) + dq_t[:, h * HD : (h + 1) * HD].T).astype(jnp.bfloat16)
-        copy = pltpu.make_async_remote_copy(
-            src_ref=gsend.at[:, cols(g * heads, heads)],
-            dst_ref=sg.at[0, :, cols(g * heads, heads)],
-            send_sem=g_s.at[g],
-            recv_sem=g_r.at[g],
-            device_id={"section": down},
-            device_id_type=MESH,
-        )
-        copy.start()
-        g_out.append(copy)
-        both = [dot(ds, qs) * scale, dot(pb, dt, NT)]
+        g_out[g].start()
+        both = [dot(ds, qs) * scale, dot(pb, dt)]
         for i in range(2):
             kvacc[i, :, cols(g)] = both[i][:HD]
             for d in range(2):
                 kvsend[d, i, :, cols(g)] = both[i][(d + 1) * HD : (d + 2) * HD].astype(jnp.bfloat16)
-        pair = [
-            pltpu.make_async_remote_copy(
-                src_ref=kvsend.at[d, :, :, cols(g)],
-                dst_ref=kvrecv.at[d, :, :, cols(g)],
-                send_sem=gkv_s.at[d, g],
-                recv_sem=gkv_r.at[d, g],
-                device_id={"seq": (before, behind)[d]},
-                device_id_type=MESH,
-            )
-            for d in range(2)
-        ]
-        pl.when(odd | has_prev)(pair[0].start)
-        pl.when(has_prev)(pair[1].start)
-        gkv_out.append(pair)
+        if parity:
+            gkv_out[g][0].start()
+        else:
+            pl.when(has_prev)(gkv_out[g][0].start)
+        pl.when(has_prev)(gkv_out[g][1].start)
 
     def project(c):
+        for a in range(tiles):
+            prune(a, c)
         at = cols(c * heads, heads)
         osend[:, at] = (x[:, at].astype(jnp.float32) + dot(att[...], w[:, at])).astype(jnp.bfloat16)
-        copy = pltpu.make_async_remote_copy(
-            src_ref=osend.at[:, at],
-            dst_ref=so.at[0, :, at],
-            send_sem=o_s.at[c],
-            recv_sem=o_r.at[c],
-            device_id={"section": up},
-            device_id_type=MESH,
+        o_out[c].start()
+
+    def run(parity, order):
+        held = {}
+        for step, g in order:
+            if step == "d":
+                attended_grad(g)
+            elif step == "e":
+                send_even()
+            elif step == "f":
+                held[g] = forward(parity, g)
+            elif step == "b":
+                backward(parity, g, *held.pop(g))
+            else:
+                project(g)
+
+    run(None, FIRST)
+    for i, copy in enumerate(wloads):
+        if i not in landed:
+            copy.wait()
+            landed.add(i)
+    loads[0].wait()
+    loads[2].wait()
+    shared = set(pruned)
+
+    @pl.when(even)
+    def _():
+        run(0, EVEN)
+
+    pruned.clear()
+    pruned.update(shared)
+
+    @pl.when(odd)
+    def _():
+        run(1, ODD)
+
+    for g in range(groups):
+        at = cols(g)
+        pl.when(even | has_next)(gkv_out[g][0].wait_recv)
+        pl.when(has_next)(gkv_out[g][1].wait_recv)
+        kvg[0, :, :, at] = (
+            kvacc[:, :, at] + kvrecv[0, :, :, at].astype(jnp.float32) + kvrecv[1, :, :, at].astype(jnp.float32)
         )
-        copy.start()
-        o_out.append(copy)
-
-    o_out, held = [], {}
-    for step, g in ORDER:
-        if step == "f":
-            held[g] = forward(g)
-        elif step == "b":
-            backward(g, *held.pop(g))
-        else:
-            project(g)
-
-    @pl.when(even | has_next)
-    def _():
-        for pair in gkv_out:
-            pair[0].wait_recv()
-
-    @pl.when(has_next)
-    def _():
-        for pair in gkv_out:
-            pair[1].wait_recv()
-
-    kvg[0] = kvacc[...] + kvrecv[0].astype(jnp.float32) + kvrecv[1].astype(jnp.float32)
 
     @pl.when(even | has_prev)
     def _():
@@ -315,9 +344,10 @@
                 pltpu.VMEM((1, rows, hid), bf),
                 pltpu.VMEM((1, 2, rows, kvw), f32),
             ),
-            in_specs=[hbm, hbm, hbm, pl.BlockSpec(memory_space=pltpu.SMEM), hbm],
+            in_specs=[hbm] * 5,
             out_specs=(vmem, vmem, vmem),
             scratch_shapes=[
+                pltpu.SMEM(mask.shape, mask.dtype),
                 pltpu.VMEM((rows, hid), bf),
                 pltpu.VMEM((rows, hid), bf),
                 pltpu.VMEM((hid, hid), bf),
@@ -330,8 +360,8 @@
                 pltpu.VMEM((2, 2, rows, kvw), bf),
                 pltpu.VMEM((2, 2, rows, kvw), bf),
                 pltpu.VMEM((2, rows, kvw), f32),
-                dma((3,)),
-                dma((groups,)),
+                dma((4,)),
+                dma((hid // HD // SLAB,)),
                 dma((2, groups)),
                 dma((2, groups)),
                 dma((2, groups)),

time: 39.9 us -> 38.2 us (0.957)
  Pallas kernels: 39.1 us -> 37.2 us
    pallas_call x1, Pallas kernels: 37.9 us -> 36.1 us  [per_device(): pl.pallas_call(functools.partial(kernel, n_seq, n_sec), out_shape=(pltpu....]
where the time goes in v3:
time: 38.2 us; the launch traced here: 38 us
  Pallas kernels  37.2 us (97%)
  between operations  0.8 us (2%)
    pallas_call x1, Pallas kernels, per_device(): pl.pallas_call(functools.partial(kernel, n_seq, n_sec), out_shape=(pltpu....  36.1 us
    pallas_call x1, Pallas kernels, per_device(): pl.pallas_call(store, out_shape=tuple((jax.ShapeDtypeStruct(o.shape, o.dt...  1.17 us

profile of v3, /device:TPU:40, one launch (start us, length us, event | category | flops | bytes accessed | tf_op | source)
XLA Modules:
  0.0 38.0 jit_solution(2280857800034572936)
XLA Ops:
  0.6 36.1 %shard_map.76 = (bf16[1,128,2048]{2,1,0:T(8,128)(2,1)S(1)}, bf16[1,128,2048]{2,1,0:T(8,128)(2,1)S(1)}, f32[1,2,128,512]{3,2,1,0:T(8,128)S(1)}) custom-call(bf16[1,128,2048]{2,1,0:T(8,128)(2,1)} %x_hbm.1, bf16[1,2,128,512]{3,2,1,0:T(8,128)(2,1)} %kv_hbm.1, bf16[1,2048,2048]{2,1,0:T(8,128)(2,1)} %w_hbm.1, s32[1,16,16]{2,1,0:T(8,128)} %mask_hbm.1, ...), custom_call_target="tpu_custom_call" | custom-call | tf_op jit(solution)/shard_map/pallas_call | solution.py:340
  36.7 1.2 %shard_map.77 = (bf16[1,128,2048]{2,1,0:T(8,128)(2,1)}, bf16[1,128,2048]{2,1,0:T(8,128)(2,1)}, f32[1,2,128,512]{3,2,1,0:T(8,128)}) custom-call(bf16[1,128,2048]{2,1,0:T(8,128)(2,1)S(1)} %get-tuple-element.6.a, bf16[1,128,2048]{2,1,0:T(8,128)(2,1)S(1)} %get-tuple-element.7.b, f32[1,2,128,512]{3,2,1,0:T(8,128)S(1)} %get-tuple-element.8.c), custom_call_target="tpu_custom_call" | custom-call | tf_op jit(solution)/shard_map/pallas_call | solution.py:378

commit v4 on v3

--- a/solution.py
+++ b/solution.py
@@ -18,6 +18,8 @@
     return [(name, int(group)) for name, group in zip(names, groups)]
 
 
+ROW = 24
+PARTS = 4
 FIRST = steps("dde", "010")
 EVEN = steps("ddfbfbfbfboooo", "23001122330123")
 ODD = steps("ffffobobdobdob", "01230011222333")
@@ -49,6 +51,8 @@
     odd = lax.rem(seq, 2) == 1
     has_next = seq + 2 < n_seq
     has_prev = seq >= 2
+    waits = (lax.rem(seq, ROW) < 2) & has_prev
+    goes = jnp.logical_not(waits)
     mate = seq + 1 - 2 * lax.rem(seq, 2)
     ahead = lax.rem(seq + 2, n_seq)
     behind = lax.rem(seq + n_seq - 2, n_seq)
@@ -80,49 +84,6 @@
         pl.when(there)(functools.partial(greet, peer))
     for peer in (up, down):
         pl.semaphore_signal(barrier, inc=1, device_id={"section": peer}, device_id_type=MESH)
-    one = [there.astype(jnp.int32) for there in (has_next, has_prev, has_cross)]
-    pl.semaphore_wait(barrier, 3 + one[0] + one[1] + one[2])
-
-    def kv_copy(d, g, src, peer):
-        return pltpu.make_async_remote_copy(
-            src_ref=src,
-            dst_ref=kvin.at[d, :, :, cols(g)],
-            send_sem=kv_s.at[d, g],
-            recv_sem=kv_r.at[d, g],
-            device_id={"seq": peer},
-            device_id_type=MESH,
-        )
-
-    direct = [kv_copy(0, g, kv_hbm.at[0, :, :, cols(g)], mate) for g in range(groups)]
-    relay = [kv_copy(0, g, kvin.at[1, :, :, cols(g)], mate) for g in range(groups)]
-    hop = [kv_copy(1, g, kv_hbm.at[0, :, :, cols(g)], ahead) for g in range(groups)]
-
-    @pl.when(odd & has_next)
-    def _():
-        for copy in hop:
-            copy.start()
-
-    @pl.when(even)
-    def _():
-        for copy in direct:
-            copy.start()
-
-    @pl.when(jnp.logical_not(has_prev))
-    def _():
-        kvin[1] = jnp.zeros(kvin.shape[1:], kvin.dtype)
-
-    @pl.when(seq == 0)
-    def _():
-        kvin[0] = jnp.zeros(kvin.shape[1:], kvin.dtype)
-
-    @pl.when(jnp.logical_not(has_next))
-    def _():
-        kvrecv[1] = jnp.zeros(kvrecv.shape[1:], kvrecv.dtype)
-
-    @pl.when(odd & jnp.logical_not(has_next))
-    def _():
-        kvrecv[0] = jnp.zeros(kvrecv.shape[1:], kvrecv.dtype)
-
     loads[3].wait()
     loads[1].wait()
     pruned, landed = set(), set()
@@ -138,12 +99,71 @@
             keep = mask[0, a, b].astype(jnp.float32).astype(jnp.bfloat16)
             w[cols(a), cols(b)] = w[cols(a), cols(b)] * keep
 
-    def attended_grad(g):
+    def attended_grad(g, keep_set=None):
         for a in range(g * heads, (g + 1) * heads):
             for c in range(groups):
                 prune(a, c)
+        if keep_set is not None:
+            pruned.clear()
+            pruned.update(keep_set)
         at = cols(g * heads, heads)
         datt[:, at] = dot(cot[...], w[at, :], NT).astype(jnp.bfloat16)
+
+    def land():
+        for i, copy in enumerate(wloads):
+            if i not in landed:
+                landed.add(i)
+                copy.wait()
+
+    @pl.when(waits)
+    def _():
+        for g in range(groups):
+            attended_grad(g)
+
+    pruned.clear()
+    landed.clear()
+    one = [there.astype(jnp.int32) for there in (has_next, has_prev, has_cross)]
+    pl.semaphore_wait(barrier, 3 + one[0] + one[1] + one[2])
+
+    def kv_copy(d, g, src, peer):
+        return pltpu.make_async_remote_copy(
+            src_ref=src,
+            dst_ref=kvin.at[d, :, :, cols(g)],
+            send_sem=kv_s.at[d, g],
+            recv_sem=kv_r.at[d, g],
+            device_id={"seq": peer},
+            device_id_type=MESH,
+        )
+
+    direct = [kv_copy(0, g, kv_hbm.at[0, :, :, cols(g)], mate) for g in range(groups)]
+    relay = [kv_copy(0, g, kvin.at[1, :, :, cols(g)], mate) for g in range(groups)]
+    hop = [kv_copy(1, g, kv_hbm.at[0, :, :, cols(g)], ahead) for g in range(groups)]
+
+    @pl.when(odd & has_next)
+    def _():
+        for copy in hop:
+            copy.start()
+
+    @pl.when(even)
+    def _():
+        for copy in direct:
+            copy.start()
+
+    @pl.when(jnp.logical_not(has_prev))
+    def _():
+        kvin[1] = jnp.zeros(kvin.shape[1:], kvin.dtype)
+
+    @pl.when(seq == 0)
+    def _():
+        kvin[0] = jnp.zeros(kvin.shape[1:], kvin.dtype)
+
+    @pl.when(jnp.logical_not(has_next))
+    def _():
+        kvrecv[1] = jnp.zeros(kvrecv.shape[1:], kvrecv.dtype)
+
+    @pl.when(odd & jnp.logical_not(has_next))
+    def _():
+        kvrecv[0] = jnp.zeros(kvrecv.shape[1:], kvrecv.dtype)
 
     def send_even():
         @pl.when(even & has_next)
@@ -252,8 +272,10 @@
     def run(parity, order):
         held = {}
         for step, g in order:
-            if step == "d":
+            if step == "d" and parity is None:
                 attended_grad(g)
+            elif step == "d":
+                pl.when(goes)(functools.partial(attended_grad, g, set(pruned)))
             elif step == "e":
                 send_even()
             elif step == "f":
@@ -263,11 +285,12 @@
             else:
                 project(g)
 
-    run(None, FIRST)
-    for i, copy in enumerate(wloads):
-        if i not in landed:
-            copy.wait()
-            landed.add(i)
+    @pl.when(goes)
+    def _():
+        run(None, FIRST)
+        land()
+
+    pl.when(waits)(send_even)
     loads[0].wait()
     loads[2].wait()
     shared = set(pruned)
@@ -316,10 +339,16 @@
 
 
 def store(a, b, c, a_out, b_out, c_out, sem):
-    copies = [
-        pltpu.make_async_copy(src, dst, sem.at[i])
-        for i, (src, dst) in enumerate([(a, a_out), (b, b_out), (c, c_out)])
-    ]
+    copies = []
+    for i, (src, dst) in enumerate([(a, a_out), (b, b_out)]):
+        part = src.shape[1] // PARTS
+        for p in range(PARTS):
+            at = pl.ds(p * part, part)
+            copies.append(pltpu.make_async_copy(src.at[:, at], dst.at[:, at], sem.at[i, p]))
+    part = c.shape[2] // PARTS
+    for p in range(PARTS):
+        at = pl.ds(p * part, part)
+        copies.append(pltpu.make_async_copy(c.at[:, :, at], c_out.at[:, :, at], sem.at[2, p]))
     for copy in copies:
         copy.start()
     for copy in copies:
@@ -380,7 +409,7 @@
             out_shape=tuple(jax.ShapeDtypeStruct(o.shape, o.dtype) for o in outs),
             in_specs=[hbm] * 3,
             out_specs=(hbm,) * 3,
-            scratch_shapes=[dma((3,))],
+            scratch_shapes=[dma((3, PARTS))],
         )(*(pltpu.with_memory_space_constraint(o, pltpu.VMEM) for o in outs))
 
     return jax.shard_map(

time: 38.2 us -> 38.4 us (level)
  no operation moved by 1% of the time
where the time goes in v4:
time: 38.4 us; the launch traced here: 38.3 us
  Pallas kernels  37.4 us (97%)
  between operations  0.82 us (2%)
    pallas_call x1, Pallas kernels, per_device(): pl.pallas_call(functools.partial(kernel, n_seq, n_sec), out_shape=(pltpu....  36.2 us
    pallas_call x1, Pallas kernels, per_device(): pl.pallas_call(store, out_shape=tuple((jax.ShapeDtypeStruct(o.shape, o.dt...  1.24 us

profile of v4, /device:TPU:40, one launch (start us, length us, event | category | flops | bytes accessed | tf_op | source)
XLA Modules:
  0.0 38.3 jit_solution(16112948655225424869)
XLA Ops:
  0.6 36.2 %shard_map.76 = (bf16[1,128,2048]{2,1,0:T(8,128)(2,1)S(1)}, bf16[1,128,2048]{2,1,0:T(8,128)(2,1)S(1)}, f32[1,2,128,512]{3,2,1,0:T(8,128)S(1)}) custom-call(bf16[1,128,2048]{2,1,0:T(8,128)(2,1)} %x_hbm.1, bf16[1,2,128,512]{3,2,1,0:T(8,128)(2,1)} %kv_hbm.1, bf16[1,2048,2048]{2,1,0:T(8,128)(2,1)} %w_hbm.1, s32[1,16,16]{2,1,0:T(8,128)} %mask_hbm.1, ...), custom_call_target="tpu_custom_call" | custom-call | tf_op jit(solution)/shard_map/pallas_call | solution.py:369
  36.9 1.2 %shard_map.77 = (bf16[1,128,2048]{2,1,0:T(8,128)(2,1)}, bf16[1,128,2048]{2,1,0:T(8,128)(2,1)}, f32[1,2,128,512]{3,2,1,0:T(8,128)}) custom-call(bf16[1,128,2048]{2,1,0:T(8,128)(2,1)S(1)} %get-tuple-element.6.a, bf16[1,128,2048]{2,1,0:T(8,128)(2,1)S(1)} %get-tuple-element.7.b, f32[1,2,128,512]{3,2,1,0:T(8,128)S(1)} %get-tuple-element.8.c), custom_call_target="tpu_custom_call" | custom-call | tf_op jit(solution)/shard_map/pallas_call | solution.py:407

commit v5 on v2

--- a/solution.py
+++ b/solution.py
@@ -11,9 +11,9 @@
 MESH = pl.DeviceIdType.MESH
 NT = (((1,), (1,)), ((), ()))
 NN = (((1,), (0,)), ((), ()))
-EVEN_AFTER = 1
+SLAB = 4
 ARRIVE = 0
-ORDER = [(step, int(g)) for step, g in zip("ffffobobobob", "012300112233")]
+ORDER = [(step, int(g)) for step, g in zip("ddekffffobobdobdob", "010001230011222333")]
 
 
 def dot(a, b, dims=NN):
@@ -26,9 +26,9 @@
 
 def kernel(
     n_seq, n_sec,
-    x_hbm, kv_hbm, w_hbm, mask, cot_hbm,
+    x_hbm, kv_hbm, w_hbm, mask_hbm, cot_hbm,
     so, sg, kvg,
-    x, cot, w, kv, kvin, datt, att, gsend, osend, kvsend, kvrecv, kvacc,
+    mask, x, cot, w, kv, kvin, datt, att, gsend, osend, kvsend, kvrecv, kvacc,
     lsem, wsem, kv_s, kv_r, gkv_s, gkv_r, g_s, g_r, o_s, o_r,
 ):
     seq, sec = lax.axis_index("seq"), lax.axis_index("section")
@@ -54,10 +54,11 @@
         pltpu.make_async_copy(kv_hbm.at[0], kv, lsem.at[0]),
         pltpu.make_async_copy(cot_hbm.at[0], cot, lsem.at[1]),
         pltpu.make_async_copy(x_hbm.at[0], x, lsem.at[2]),
+        pltpu.make_async_copy(mask_hbm, mask, lsem.at[3]),
     ]
     wloads = [
-        pltpu.make_async_copy(w_hbm.at[0, cols(g * heads, heads)], w.at[cols(g * heads, heads)], wsem.at[g])
-        for g in range(groups)
+        pltpu.make_async_copy(w_hbm.at[0, cols(i * SLAB, SLAB)], w.at[cols(i * SLAB, SLAB)], wsem.at[i])
+        for i in range(tiles // SLAB)
     ]
     for copy in loads + wloads:
         copy.start()
@@ -115,25 +116,34 @@
     def _():
         kvrecv[0] = jnp.zeros(kvrecv.shape[1:], kvrecv.dtype)
 
+    loads[3].wait()
     loads[1].wait()
-    cot_v = cot[...]
-    for g in range(groups):
-        wloads[g].wait()
+    pruned, landed = set(), set()
+
+    def prune(a, c):
+        if a // SLAB not in landed:
+            landed.add(a // SLAB)
+            wloads[a // SLAB].wait()
+        if (a, c) in pruned:
+            return
+        pruned.add((a, c))
+        for b in range(c * heads, (c + 1) * heads):
+            keep = mask[0, a, b].astype(jnp.float32).astype(jnp.bfloat16)
+            w[cols(a), cols(b)] = w[cols(a), cols(b)] * keep
+
+    def attended_grad(g):
         for a in range(g * heads, (g + 1) * heads):
-            for b in range(tiles):
-                keep = mask[0, a, b].astype(jnp.float32).astype(jnp.bfloat16)
-                w[cols(a), cols(b)] = w[cols(a), cols(b)] * keep
-        full = dot(w[cols(g * heads, heads), :], cot_v, NT).astype(jnp.bfloat16)
-        for h in range(heads):
-            datt[:, cols(g * heads + h)] = full[h * HD : (h + 1) * HD]
-        if g == EVEN_AFTER:
-            @pl.when(even & has_next)
-            def _():
-                for copy in hop:
-                    copy.start()
-
-    loads[0].wait()
-    loads[2].wait()
+            for c in range(groups):
+                prune(a, c)
+        at = cols(g * heads, heads)
+        datt[:, at] = dot(cot[...], w[at, :], NT).astype(jnp.bfloat16)
+
+    def send_even():
+        @pl.when(even & has_next)
+        def _():
+            for copy in hop:
+                copy.start()
+
     key = lax.broadcasted_iota(jnp.int32, (HD, width), 0)
     tok = lax.broadcasted_iota(jnp.int32, (HD, width), 1) % HD
     own = key <= tok
@@ -188,8 +198,8 @@
         return ks, vs, qs, pc, p1, pb
 
     def backward(g, ks, vs, qs, pc, p1, pb):
-        dt = datt[:, cols(g * heads, heads)]
-        dp = dot(vs, dt)
+        dt = jnp.concatenate([datt[:, cols(g * heads + h)] for h in range(heads)], axis=0)
+        dp = dot(vs, dt, NT)
         dc, d1 = jnp.where(own, dp[:HD], dp[2 * HD :]), dp[HD : 2 * HD]
         row = jnp.sum(pc * dc, axis=0, keepdims=True) + jnp.sum(p1 * d1, axis=0, keepdims=True)
         ds = split((pc * (dc - row)).astype(jnp.bfloat16), (p1 * (d1 - row)).astype(jnp.bfloat16))
@@ -207,7 +217,7 @@
         )
         copy.start()
         g_out.append(copy)
-        both = [dot(ds, qs) * scale, dot(pb, dt, NT)]
+        both = [dot(ds, qs) * scale, dot(pb, dt)]
         for i in range(2):
             kvacc[i, :, cols(g)] = both[i][:HD]
             for d in range(2):
@@ -228,6 +238,8 @@
         gkv_out.append(pair)
 
     def project(c):
+        for a in range(tiles):
+            prune(a, c)
         at = cols(c * heads, heads)
         osend[:, at] = (x[:, at].astype(jnp.float32) + dot(att[...], w[:, at])).astype(jnp.bfloat16)
         copy = pltpu.make_async_remote_copy(
@@ -243,7 +255,14 @@
 
     o_out, held = [], {}
     for step, g in ORDER:
-        if step == "f":
+        if step == "k":
+            loads[0].wait()
+            loads[2].wait()
+        elif step == "d":
+            attended_grad(g)
+        elif step == "e":
+            send_even()
+        elif step == "f":
             held[g] = forward(g)
         elif step == "b":
             backward(g, *held.pop(g))
@@ -315,9 +334,10 @@
                 pltpu.VMEM((1, rows, hid), bf),
                 pltpu.VMEM((1, 2, rows, kvw), f32),
             ),
-            in_specs=[hbm, hbm, hbm, pl.BlockSpec(memory_space=pltpu.SMEM), hbm],
+            in_specs=[hbm] * 5,
             out_specs=(vmem, vmem, vmem),
             scratch_shapes=[
+                pltpu.SMEM(mask.shape, mask.dtype),
                 pltpu.VMEM((rows, hid), bf),
                 pltpu.VMEM((rows, hid), bf),
                 pltpu.VMEM((hid, hid), bf),
@@ -330,8 +350,8 @@
                 pltpu.VMEM((2, 2, rows, kvw), bf),
                 pltpu.VMEM((2, 2, rows, kvw), bf),
                 pltpu.VMEM((2, rows, kvw), f32),
-                dma((3,)),
-                dma((groups,)),
+                dma((4,)),
+                dma((hid // HD // SLAB,)),
                 dma((2, groups)),
                 dma((2, groups)),
                 dma((2, groups)),

time: 39.9 us -> 37.8 us (0.947)
  the two profiles are of different devices: /device:TPU:40 before, /device:TPU:46 now
where the time goes in v5:
time: 37.8 us; the launch traced here: 37.7 us
  Pallas kernels  37 us (98%)
  between operations  0.64 us (2%)
    pallas_call x1, Pallas kernels, per_device(): pl.pallas_call(functools.partial(kernel, n_seq, n_sec), out_shape=(pltpu....  35.9 us
    pallas_call x1, Pallas kernels, per_device(): pl.pallas_call(store, out_shape=tuple((jax.ShapeDtypeStruct(o.shape, o.dt...  1.17 us

profile of v5, /device:TPU:46, one launch (start us, length us, event | category | flops | bytes accessed | tf_op | source)
XLA Modules:
  0.0 37.7 jit_solution(9349746410271136857)
XLA Ops:
  0.6 35.9 %shard_map.76 = (bf16[1,128,2048]{2,1,0:T(8,128)(2,1)S(1)}, bf16[1,128,2048]{2,1,0:T(8,128)(2,1)S(1)}, f32[1,2,128,512]{3,2,1,0:T(8,128)S(1)}) custom-call(bf16[1,128,2048]{2,1,0:T(8,128)(2,1)} %x_hbm.1, bf16[1,2,128,512]{3,2,1,0:T(8,128)(2,1)} %kv_hbm.1, bf16[1,2048,2048]{2,1,0:T(8,128)(2,1)} %w_hbm.1, s32[1,16,16]{2,1,0:T(8,128)} %mask_hbm.1, ...), custom_call_target="tpu_custom_call" | custom-call | tf_op jit(solution)/shard_map/pallas_call | solution.py:330
  36.5 1.2 %shard_map.77 = (bf16[1,128,2048]{2,1,0:T(8,128)(2,1)}, bf16[1,128,2048]{2,1,0:T(8,128)(2,1)}, f32[1,2,128,512]{3,2,1,0:T(8,128)}) custom-call(bf16[1,128,2048]{2,1,0:T(8,128)(2,1)S(1)} %get-tuple-element.6.a, bf16[1,128,2048]{2,1,0:T(8,128)(2,1)S(1)} %get-tuple-element.7.b, f32[1,2,128,512]{3,2,1,0:T(8,128)S(1)} %get-tuple-element.8.c), custom_call_target="tpu_custom_call" | custom-call | tf_op jit(solution)/shard_map/pallas_call | solution.py:368
